TPU v7x, 32 devices: a whole 2x2x4 slice. The times are simulated.
32 devices in a mesh: grp: 2 (over y), seq: 4 (over z), head: 2 (over x), dat: 2 (over core).
Axes of the slice: x: 2, y: 2, z: 4, core: 2. Of those that a mesh axis runs over, the one named last changes fastest.
Arguments:
- queries: bfloat16 [4, 256, 3072], P(('grp', 'dat'), 'seq', 'head'), parts along dimension 0, may hold values from -10 to 10
- keys: bfloat16 [4, 256, 512], P(('grp', 'dat'), 'seq', 'head'), parts along dimension 0, may hold values from -6 to 6
- values: bfloat16 [4, 256, 512], P(('grp', 'dat'), 'seq', 'head'), parts along dimension 0, may hold values from -6 to 6
- residual_in: bfloat16 [4, 256, 3072], P(('grp', 'dat'), 'seq', 'head'), parts along dimension 0, may hold values from -40 to 40
- out_proj: bfloat16 [24, 128, 3072], P('head', 'seq'), may hold values from -0.5 to 0.5
- norm_gain: bfloat16 [3072], replicated, may hold values from 0.5 to 1.5
- expert_gate: bfloat16 [4, 3072, 8192], P('head', None, 'seq'), may hold values from -0.109375 to 0.109375
- expert_up: bfloat16 [4, 3072, 8192], P('head', None, 'seq'), may hold values from -0.109375 to 0.109375
- routes: int32 [4, 256, 2], P(('grp', 'dat'), 'seq'), parts along dimension 0, may hold values from 0 to 3, as said below
- gate_numer: int32 [4, 256], P(('grp', 'dat'), 'seq'), parts along dimension 0, may hold values from 64 to 191
- sequence_lengths: int32 [4], P(('grp', 'dat')), parts along dimension 0, may hold values from 128 to 256, as said below
Outputs:
- stream: bfloat16 [4, 256, 3072], P(('grp', 'dat'), 'seq', 'head'), parts along dimension 0
- expert_hidden: bfloat16 [4, 4, 160, 8192], P('head', ('grp', 'dat'), None, 'seq'), parts along dimension 1
There are 2 independent parts, one for each index of `grp`. A program takes and returns all parts, laid end to end along the dimension named above; an argument that names none is the same for every part. Nothing has to cross between parts.
Inputs may be any that keep to these rules, and one draw needn't show every extreme that they name: `routes`: for each sequence one expert is named by exactly 40 tokens of every aligned block of 64 positions, every other expert by at most 40 tokens of such a block; the two experts of a token differ. `sequence_lengths`: one sequence of the batch has the full length 256.
All inputs are finite; a program needn't handle non-finite values.
Results may differ from a plain program's by a relative error of at most 0.019.
Values may be sent and summed in bfloat16 or wider, within the bound.
A program may use at most 128 MiB of HBM per device.

v0:
```python
import math

import jax
import jax.numpy as jnp
from jax import lax
from jax.sharding import PartitionSpec as P

D = 3072
QUERY_HEAD_COUNT = 24
KEY_VALUE_HEADS = 4
HEAD_SIZE = 128
MOST = 40


EPS = 1e-05
NEG = -1e30


def slot_sources(marked, capacity):
    tok_len = marked.shape[1]
    counted = jnp.cumsum(marked, axis=1)
    rank_ids = jnp.arange(capacity, dtype=jnp.int32)
    source = jnp.sum((counted[:, None, :] <= rank_ids[None, :, None]).astype(jnp.int32), axis=2)
    filled = rank_ids[None, :] < counted[:, -1:]
    source = jnp.minimum(source, tok_len - 1)
    return (source, filled)


def expert_rows(rows_in, slot_gate, gate_matrix, up_matrix):
    gate_part = jnp.dot(rows_in, gate_matrix, preferred_element_type=jnp.float32)
    up_part = jnp.dot(rows_in, up_matrix, preferred_element_type=jnp.float32)
    return (slot_gate[:, None] * (jax.nn.silu(gate_part) * up_part)).astype(jnp.bfloat16)


def local(
    queries,
    keys,
    values,
    residual_in,
    out_proj,
    norm_gain,
    expert_gate,
    expert_up,
    routes,
    gate_numer,
    sequence_lengths,
):
    tok_count = queries.shape[1]
    kv_local = keys.shape[2] // HEAD_SIZE
    heads_per_group = QUERY_HEAD_COUNT // KEY_VALUE_HEADS
    seq_rank = lax.axis_index("seq")
    head_rank = lax.axis_index("head")
    query_pos = seq_rank * tok_count + jnp.arange(tok_count, dtype=jnp.int32)
    valid_len = sequence_lengths[0]
    score_scale = 1.0 / math.sqrt(HEAD_SIZE)
    query_heads = queries[0].reshape(tok_count, kv_local, heads_per_group, HEAD_SIZE)
    top_score = jnp.full((kv_local, heads_per_group, tok_count), NEG, jnp.float32)
    key_part = lax.all_gather(keys, "seq", axis=1, tiled=True)
    value_part = lax.all_gather(values, "seq", axis=1, tiled=True)
    part_len = key_part.shape[1]
    key_heads = key_part[0].reshape(part_len, kv_local, HEAD_SIZE)
    value_heads = value_part[0].reshape(part_len, kv_local, HEAD_SIZE)
    scores = (
        jnp.einsum("tghd,ngd->ghtn", query_heads, key_heads, preferred_element_type=jnp.float32)
        * score_scale
    )
    key_pos = jnp.arange(part_len, dtype=jnp.int32)
    allowed = (key_pos[None, :] <= query_pos[:, None]) & (key_pos < valid_len)[None, :]
    scores = jnp.where(allowed, scores, NEG)
    new_top = jnp.maximum(top_score, jnp.max(scores, axis=-1))
    weights = jnp.where(allowed, jnp.exp(scores - new_top[..., None]), 0.0)
    denom_sum = jnp.sum(weights, axis=-1)
    weighted = jnp.einsum(
        "ghtn,ngd->ghtd",
        weights.astype(jnp.bfloat16),
        value_heads,
        preferred_element_type=jnp.float32,
    )
    top_score, denom_sum, weighted = (new_top, denom_sum, weighted)
    attended_values = (weighted / denom_sum[..., None]).astype(jnp.bfloat16)
    attn_heads = attended_values.transpose(2, 0, 1, 3).reshape(
        tok_count, kv_local * heads_per_group, HEAD_SIZE
    )
    proj_part = lax.all_gather(out_proj, "seq", axis=1, tiled=True)
    mixed_sum = jnp.einsum("thd,hdc->tc", attn_heads, proj_part, preferred_element_type=jnp.float32)
    share_width = residual_in.shape[2]
    col_start = head_rank * share_width
    own_input = residual_in[0].astype(jnp.float32)
    shared = lax.psum_scatter(
        mixed_sum.astype(jnp.bfloat16), "head", scatter_dimension=1, tiled=True
    ).astype(jnp.float32)
    stream_share = (own_input + shared).astype(jnp.bfloat16)
    as_float = stream_share.astype(jnp.float32)
    squares = lax.psum(jnp.sum(as_float * as_float, axis=1, keepdims=True), "head")
    gain_part = lax.dynamic_slice_in_dim(norm_gain, col_start, share_width, 0).astype(jnp.float32)
    normed_part = (as_float * lax.rsqrt(squares / D + EPS) * gain_part).astype(jnp.bfloat16)
    normed = lax.all_gather(normed_part, "head", axis=1, tiled=True)
    local_experts = expert_gate.shape[0]
    expert_ids = head_rank * local_experts + jnp.arange(local_experts, dtype=jnp.int32)
    first_weight = gate_numer[0].astype(jnp.float32) / 256.0
    route_first = routes[0, :, 0]
    route_second = routes[0, :, 1]
    token_gates = jnp.where(
        route_first[:, None] == expert_ids[None, :], first_weight[:, None], 0.0
    ) + jnp.where(route_second[:, None] == expert_ids[None, :], 1.0 - first_weight[:, None], 0.0)
    capacity = MOST
    packed_rows = []
    packed_gates = []
    for expert_slot in range(local_experts):
        marked = (token_gates[:, expert_slot] > 0).astype(jnp.int32)[None, :]
        source, filled = slot_sources(marked, capacity)
        packed_rows.append(jnp.take(normed, source[0], axis=0))
        packed_gates.append(
            jnp.where(filled[0], jnp.take(token_gates[:, expert_slot], source[0]), 0.0).astype(
                jnp.bfloat16
            )
        )
    stacked_rows = jnp.stack(packed_rows)
    stacked_gates = jnp.stack(packed_gates)
    rows_out, gates_out = (
        lax.all_gather(stacked_rows, "seq", axis=1, tiled=True),
        lax.all_gather(stacked_gates, "seq", axis=1, tiled=True),
    )
    outputs = []
    for expert_slot in range(local_experts):
        outputs.append(
            expert_rows(
                rows_out[expert_slot],
                gates_out[expert_slot].astype(jnp.float32),
                expert_gate[expert_slot],
                expert_up[expert_slot],
            )
        )
    hidden = jnp.stack(outputs)
    return (stream_share[None], hidden[:, None])


def solution(mesh):
    in_specs = (
        P(("grp", "dat"), "seq", "head"),
        P(("grp", "dat"), "seq", "head"),
        P(("grp", "dat"), "seq", "head"),
        P(("grp", "dat"), "seq", "head"),
        P("head", "seq", None),
        P(),
        P("head", None, "seq"),
        P("head", None, "seq"),
        P(("grp", "dat"), "seq", None),
        P(("grp", "dat"), "seq"),
        P(("grp", "dat")),
    )
    out_specs = (P(("grp", "dat"), "seq", "head"), P("head", ("grp", "dat"), None, "seq"))
    return jax.shard_map(local, mesh=mesh, in_specs=in_specs, out_specs=out_specs, check_vma=False)
```

profile of v0, /device:TPU:20, one launch (start us, length us, event | category | flops | bytes accessed | tf_op | source)
XLA Modules:
  0.0 290.8 jit_solution(12492824044068273958)
XLA Ops:
  7.3 0.7 all-gather.4.cloned.1.call-update
  8.7 11.6 %all_gather.18 = bf16[1,256,256]{2,1,0:T(8,128)(2,1)S(1)} all-gather(bf16[1,64,256]{2,1,0:T(8,128)(2,1)S(1)} %copy-done.2), channel_id=1, replica_groups=mesh['grp'=2,'seq'=4,'head'=2,'dat'=2] {'seq'}, dimensions={1}, use_global_device_ids=true | all-gather | bytes 163840 | tf_op jit(solution)/shard_map/all_gather | solution.py:58
  20.4 0.2 reshape_squeeze.10
  20.7 19.9 %all_gather.19 = bf16[1,256,256]{2,1,0:T(8,128)(2,1)S(1)} all-gather(bf16[1,64,256]{2,1,0:T(8,128)(2,1)S(1)} %copy-done.3), channel_id=1, replica_groups=mesh['grp'=2,'seq'=4,'head'=2,'dat'=2] {'seq'}, dimensions={1}, use_global_device_ids=true | all-gather | bytes 163840 | tf_op jit(solution)/shard_map/all_gather | solution.py:59
  40.9 0.2 reduce_window_sum.17
  41.1 0.2 reduce_window_sum.18
  41.6 0.3 fusion.62
  41.9 0.3 fusion.41
  42.2 0.3 fusion.40
  42.6 135.0 %all-gather.4.cloned.1.call-done = bf16[12,128,3072]{2,1,0:T(8,128)(2,1)} async-done(((bf16[12,32,3072]{2,1,0:T(8,128)(2,1)}), bf16[12,128,3072]{2,1,0:T(8,128)(2,1)}) %all-gather.4.cloned.1.call-update) | async-done | bytes 9437200 | tf_op jit(solution)/shard_map/all_gather | solution.py:84
  177.6 6.2 %fusion.12 = bf16[64,3072]{1,0:T(8,128)(2,1)} fusion(bf16[64,12,128]{2,0,1:T(8,128)(2,1)S(1)} %bitcast.128, bf16[12,128,3072]{2,1,0:T(8,128)(2,1)} %all-gather.4.cloned.1.call-done), kind=kOutput, calls=%fused_computation.17 | convolution fusion | flops 604176384 | bytes 10027008 | tf_op jit(solution)/shard_map/thd,hdc->tc/dot_general | solution.py:85
  184.2 13.1 %reduce-scatter.2.cloned.1.call-done = bf16[64,1536]{1,0:T(8,128)(2,1)} async-done(((bf16[64,3072]{1,0:T(8,128)(2,1)}), bf16[64,1536]{1,0:T(8,128)(2,1)}) %reduce-scatter.2.cloned.1.call-update) | async-done | bytes 196624 | tf_op jit(solution)/shard_map/reduce_scatter | solution.py:89
  197.3 1.1 fusion.43
  198.4 4.9 %psum.7 = f32[64,1]{0,1:T(1,128)S(1)} all-reduce(f32[64,1]{0,1:T(1,128)S(1)} %bitcast.134), channel_id=1, replica_groups=mesh['grp'=2,'seq'=4,'head'=2,'dat'=2] {'head'}, use_global_device_ids=true, to_apply=%region_8.10 | all-reduce | flops 64 | bytes 512 | tf_op jit(solution)/shard_map/psum | solution.py:94
  203.4 1.7 fusion.45
  205.0 6.3 %all_gather.22 = bf16[64,3072]{1,0:T(8,128)(2,1)S(1)} all-gather(bf16[64,1536]{1,0:T(8,128)(2,1)S(1)} %get-tuple-element.16), channel_id=1, replica_groups=mesh['grp'=2,'seq'=4,'head'=2,'dat'=2] {'head'}, dimensions={1}, use_global_device_ids=true | all-gather | bytes 589824 | tf_op jit(solution)/shard_map/all_gather | solution.py:97
  211.3 0.7 gather_fusion.2
  212.0 0.7 gather_fusion.3
  212.7 0.1 select_bitcast_fusion
  212.9 0.8 pad_maximum_fusion
  213.7 0.6 slice.47
  214.4 0.6 slice.49
  215.0 0.8 gather_fusion
  215.8 0.8 gather_fusion.1
  216.5 1.2 fusion.56
  217.8 8.4 %all-gather = bf16[4,40,2]{1,2,0:T(2,128)(2,1)S(1)} all-gather(bf16[1,40,2]{1,2,0:T(2,128)(2,1)S(1)} %maximum_bitcast_fusion.1), channel_id=1, replica_groups=mesh['grp'=2,'seq'=4,'head'=2,'dat'=2] {'seq'}, dimensions={0}, use_global_device_ids=true | all-gather | bytes 800 | tf_op jit(solution)/shard_map/all_gather | solution.py:122
  226.3 29.9 %all-gather.6.cloned.1.call-done = bf16[2,160,3072]{2,1,0:T(8,128)(2,1)} async-done(((bf16[2,40,3072]{2,1,0:T(8,128)(2,1)}), bf16[2,160,3072]{2,1,0:T(8,128)(2,1)}) %all-gather.6.cloned.1.call-update) | async-done | bytes 1966096 | tf_op jit(solution)/shard_map/all_gather | solution.py:121
  256.2 7.0 %fusion.6 = f32[160,2048]{1,0:T(8,128)S(1)} fusion(bf16[2,3072,2048]{2,1,0:T(8,128)(2,1)} %param.21, bf16[2,160,3072]{2,1,0:T(8,128)(2,1)} %all-gather.6.cloned.1.call-done), kind=kOutput, calls=%fused_computation.10 | convolution fusion | flops 2013265920 | bytes 14876672 | tf_op jit(solution)/shard_map/dot_general | solution.py:30
  263.3 5.8 %fusion.2 = f32[160,2048]{1,0:T(8,128)S(1)} fusion(bf16[2,3072,2048]{2,1,0:T(8,128)(2,1)} %param.21, bf16[2,160,3072]{2,1,0:T(8,128)(2,1)S(1)} %copy-done.6), kind=kOutput, calls=%fused_computation.6 | convolution fusion | flops 2013265920 | bytes 14876672 | tf_op jit(solution)/shard_map/dot_general | solution.py:30
  269.1 7.0 %fusion.31 = bf16[1,160,2048]{2,1,0:T(8,128)(2,1)S(1)} fusion(bf16[2,3072,2048]{2,1,0:T(8,128)(2,1)} %param.22, f32[160,2048]{1,0:T(8,128)S(1)} %fusion.6, bf16[2,160,3072]{2,1,0:T(8,128)(2,1)S(1)} %copy-done.6, f32[160]{0:T(256)S(1)} %bitcast.133), kind=kOutput, calls=%fused_computation.24 | convolution fusion | flops 2015559680 | bytes 15533056 | tf_op jit(solution)/shard_map/dot_general | solution.py:31
  276.1 7.0 %fusion.34 = bf16[1,160,2048]{2,1,0:T(8,128)(2,1)S(1)} fusion(bf16[2,3072,2048]{2,1,0:T(8,128)(2,1)} %param.22, f32[160,2048]{1,0:T(8,128)S(1)} %fusion.2, bf16[2,160,3072]{2,1,0:T(8,128)(2,1)S(1)} %copy-done.6, f32[160]{0:T(256)S(1)} %bitcast.132), kind=kOutput, calls=%fused_computation.25 | convolution fusion | flops 2015559680 | bytes 15533056 | tf_op jit(solution)/shard_map/dot_general | solution.py:31
  283.1 1.2 maximum_bitcast_fusion
  (46 shorter events, 1.0 us)
Async XLA Ops:
  7.2 1.5 copy-start.2
  7.2 13.2 %copy-start.1 = (bf16[1,64,1536]{2,1,0:T(8,128)(2,1)S(1)}, bf16[1,64,1536]{2,1,0:T(8,128)(2,1)}, u32[]{:S(2)}) copy-start(bf16[1,64,1536]{2,1,0:T(8,128)(2,1)} %param.15) | copy-start | bytes 589828
  7.2 13.5 %copy-start.3 = (bf16[1,64,256]{2,1,0:T(8,128)(2,1)S(1)}, bf16[1,64,256]{2,1,0:T(8,128)(2,1)}, u32[]{:S(2)}) copy-start(bf16[1,64,256]{2,1,0:T(8,128)(2,1)} %param.17) | copy-start | bytes 98308
  7.2 33.5 %copy-start.7 = (s32[1,64]{1,0:T(1,128)S(1)}, s32[1,64]{1,0:T(1,128)}, u32[]{:S(2)}) copy-start(s32[1,64]{1,0:T(1,128)} %param.24) | copy-start | bytes 772
  7.2 33.5 %copy-start.5 = (s32[1,64,2]{1,2,0:T(2,128)S(1)}, s32[1,64,2]{1,2,0:T(2,128)}, u32[]{:S(2)}) copy-start(s32[1,64,2]{1,2,0:T(2,128)} %param.23) | copy-start | bytes 1540
  7.2 170.4 %all-gather.4.cloned.1.call-start = ((), (), s32[]{:S(2)}) async-start(), calls=%async_computation.1 | async-start | bytes 11796480 | tf_op jit(solution)/shard_map/all_gather | solution.py:84
  7.9 189.4 %reduce-scatter.2.cloned.1.call-start = ((), (), s32[]{:S(2)}) async-start(), calls=%async_computation.2 | async-start | bytes 589824 | tf_op jit(solution)/shard_map/reduce_scatter | solution.py:89
  177.6 6.5 %copy-start.4 = (bf16[3072]{0:T(1024)(128)(2,1)S(1)}, bf16[3072]{0:T(1024)(128)(2,1)}, u32[]{:S(2)}) copy-start(bf16[3072]{0:T(1024)(128)(2,1)} %param.20) | copy-start | bytes 18436
  177.6 19.7 %copy-start = (bf16[1,64,1536]{2,1,0:T(8,128)(2,1)S(1)}, bf16[1,64,1536]{2,1,0:T(8,128)(2,1)}, u32[]{:S(2)}) copy-start(bf16[1,64,1536]{2,1,0:T(8,128)(2,1)} %param.18) | copy-start | bytes 589828
  183.9 72.3 %all-gather.6.cloned.1.call-start = ((), (), s32[]{:S(2)}) async-start(), calls=%async_computation.3 | async-start | bytes 2457600 | tf_op jit(solution)/shard_map/all_gather | solution.py:121
  256.2 7.0 %copy-start.6 = (bf16[2,160,3072]{2,1,0:T(8,128)(2,1)S(1)}, bf16[2,160,3072]{2,1,0:T(8,128)(2,1)}, u32[]{:S(2)}) copy-start(bf16[2,160,3072]{2,1,0:T(8,128)(2,1)} %all-gather.6.cloned.1.call-done) | copy-start | bytes 5898244
Sparse Core Ops, SparseCore 0:
  9.6 167.9 all-gather.3
  184.0 13.2 reduce-scatter.1
  213.8 42.3 all-gather.5
where the time goes:
time: 294 us; the launch traced here: 291 us
  waiting for transfers between devices  179 us (61%)
  blocking collectives  51.2 us (17%)
  matrix products  33.7 us (11%)
  between operations  14.7 us (5%)
  other arithmetic  7.48 us (3%)
  local copies, waits for them, and re-layouts  4.78 us (2%)
    all_gather x1, waiting for transfers between devices, local(): proj_part = lax.all_gather(out_proj, 'seq', axis=1, tiled=True)  135 us
    all_gather x1, waiting for transfers between devices, local(): lax.all_gather(stacked_rows, 'seq', axis=1, tiled=True)  29.9 us
    all_gather x1, blocking collectives, local(): value_part = lax.all_gather(values, 'seq', axis=1, tiled=True)  19.9 us
    dot_general x2, matrix products, expert_rows(): up_part = jnp.dot(rows_in, up_matrix, preferred_element_type=jnp.float32)  14 us
    reduce_scatter x1, waiting for transfers between devices, local(): lax.psum_scatter(mixed_sum.astype(jnp.bfloat16), 'head', scatter_dimensio...  13.1 us
    dot_general x2, matrix products, expert_rows(): jnp.dot(rows_in, gate_matrix, preferred_element_type=jnp.float32)  12.9 us
    all_gather x1, blocking collectives, local(): key_part = lax.all_gather(keys, 'seq', axis=1, tiled=True)  11.6 us
    all_gather x1, blocking collectives, local(): lax.all_gather(stacked_gates, 'seq', axis=1, tiled=True)  8.39 us
  transfers between devices with their start and end apart: 3, of which 3 were waited for; matrix products, arithmetic and copies ran while one was open for 2% of the time, Pallas kernels for 0%

commit v1 on v0

v1 whole, which is shorter than its diff:
```python
import functools
import math

import jax
import jax.numpy as jnp
from jax import lax
from jax.experimental import pallas as pl
from jax.experimental.pallas import tpu as pltpu
from jax.sharding import PartitionSpec as P

HEAD_SIZE = 128
MOST = 40
EPS = 1e-05
NEG = -1e30
MESH = pl.DeviceIdType.MESH
F32 = jnp.float32
BF16 = jnp.bfloat16


def mix_kernel(
    n, m, nd,
    len_ref, q_ref, k_ref, v_ref, meta_ref, res_ref, w_ref,
    st_ref, own_ref, metas_ref,
    kbuf, vbuf, wbuf, cut, abuf, part, rbuf,
    k_s, k_r, v_s, v_r, me_s, me_r, w_s, w_r, wf_s, wf_r, wl,
    a_s, a_r, af_s, af_r, r_s, r_r, t_s, t_r, tx_s, tx_r,
):
    z = lax.axis_index("seq")
    x = lax.axis_index("head")
    c = lax.axis_index("dat")
    tok = q_ref.shape[0]
    heads = q_ref.shape[1] // HEAD_SIZE
    groups = k_ref.shape[1] // HEAD_SIZE
    per = heads // groups
    width = HEAD_SIZE // n
    share = res_ref.shape[1]
    wide = share // nd

    def peer(me, k, size):
        return lax.rem(me + k, size)

    def source(me, k, size):
        return lax.rem(me - k + size, size)

    sends = []

    def send(src, dst, s_sem, r_sem, where):
        copy = pltpu.make_async_remote_copy(
            src_ref=src, dst_ref=dst, send_sem=s_sem, recv_sem=r_sem,
            device_id=where, device_id_type=MESH,
        )
        copy.start()
        sends.append(copy)

    def arrived(dst, s_sem, r_sem, where):
        pltpu.make_async_remote_copy(
            src_ref=dst, dst_ref=dst, send_sem=s_sem, recv_sem=r_sem,
            device_id=where, device_id_type=MESH,
        ).wait_recv()

    barrier = pltpu.get_barrier_semaphore()
    for axis, me, size in (("seq", z, n), ("head", x, m), ("dat", c, nd)):
        for k in range(1, size):
            pl.semaphore_signal(barrier, inc=1, device_id={axis: peer(me, k, size)}, device_id_type=MESH)
    local_w = []
    for i in range(nd):
        start = pl.multiple_of(x * share + i * wide, 128)
        local = pltpu.make_async_copy(w_ref.at[:, pl.ds(start, wide)], wbuf.at[x, i], wl.at[i])
        local.start()
        local_w.append(local)
    pl.semaphore_wait(barrier, n - 1 + m - 1 + nd - 1)

    for k in range(1, n):
        to = {"seq": peer(z, k, n)}
        send(k_ref, kbuf.at[z], k_s.at[k - 1], k_r.at[k - 1], to)
        send(v_ref, vbuf.at[z], v_s.at[k - 1], v_r.at[k - 1], to)
    for j in range(1, m):
        to = peer(x, j, m)
        start = pl.multiple_of(to * share + c * wide, 128)
        send(w_ref.at[:, pl.ds(start, wide)], wbuf.at[x, c], w_s.at[j - 1], w_r.at[j - 1], {"head": to})
    for k in range(1, n):
        send(meta_ref, metas_ref.at[z], me_s.at[k - 1], me_r.at[k - 1], {"seq": peer(z, k, n)})
    kbuf[z] = k_ref[...]
    vbuf[z] = v_ref[...]
    metas_ref[z] = meta_ref[...]

    for k in range(1, n):
        s = source(z, k, n)
        arrived(kbuf.at[s], k_s.at[k - 1], k_r.at[k - 1], {"seq": s})
        arrived(vbuf.at[s], v_s.at[k - 1], v_r.at[k - 1], {"seq": s})

    row = lax.broadcasted_iota(jnp.int32, (per * tok, n * tok), 0)
    col = lax.broadcasted_iota(jnp.int32, (per * tok, n * tok), 1)
    allowed = (col <= lax.rem(row, tok) + z * tok) & (col < len_ref[0])
    scale = 1.0 / math.sqrt(HEAD_SIZE)
    done = []
    for g in range(groups):
        lanes = slice(g * HEAD_SIZE, (g + 1) * HEAD_SIZE)
        queries = jnp.concatenate(
            [q_ref[:, (g * per + i) * HEAD_SIZE : (g * per + i + 1) * HEAD_SIZE] for i in range(per)], axis=0
        )
        keys = kbuf[:, :, lanes].reshape(n * tok, HEAD_SIZE)
        vals = vbuf[:, :, lanes].reshape(n * tok, HEAD_SIZE)
        scores = lax.dot_general(queries, keys, (((1,), (1,)), ((), ())), preferred_element_type=F32) * scale
        scores = jnp.where(allowed, scores, NEG)
        top = jnp.max(scores, axis=1, keepdims=True)
        probs = jnp.where(allowed, jnp.exp(scores - top), 0.0)
        denom = jnp.sum(probs, axis=1, keepdims=True)
        mixed = jnp.dot(probs.astype(BF16), vals, preferred_element_type=F32)
        done.append((mixed / denom).astype(BF16))
    for d in range(n):
        cut[d] = jnp.concatenate(
            [
                done[g][i * tok : (i + 1) * tok, d * width : (d + 1) * width]
                for g in range(groups)
                for i in range(per)
            ],
            axis=1,
        )
    for k in range(1, n):
        to = peer(z, k, n)
        send(cut.at[to], abuf.at[x, z], a_s.at[k - 1], a_r.at[k - 1], {"seq": to})
    for j in range(1, m):
        send(cut.at[z], abuf.at[x, z], af_s.at[j - 1, 0], af_r.at[j - 1, 0], {"head": peer(x, j, m)})
    abuf[x, z] = cut[z]
    for j in range(1, m):
        s = source(x, j, m)
        arrived(wbuf.at[s, c], w_s.at[j - 1], w_r.at[j - 1], {"head": s})
        for i in range(1, nd):
            send(wbuf.at[s, c], wbuf.at[s, c], wf_s.at[j - 1, i - 1], wf_r.at[j - 1, i - 1], {"dat": peer(c, i, nd)})
    for k in range(1, n):
        s = source(z, k, n)
        arrived(abuf.at[x, s], a_s.at[k - 1], a_r.at[k - 1], {"seq": s})
        for j in range(1, m):
            send(abuf.at[x, s], abuf.at[x, s], af_s.at[j - 1, k], af_r.at[j - 1, k], {"head": peer(x, j, m)})
    for local in local_w:
        local.wait()
    for j in range(1, m):
        s = source(x, j, m)
        for i in range(1, nd):
            d = source(c, i, nd)
            arrived(wbuf.at[s, d], wf_s.at[j - 1, i - 1], wf_r.at[j - 1, i - 1], {"dat": d})
        for k in range(n):
            b = source(z, k, n)
            arrived(abuf.at[s, b], af_s.at[j - 1, k], af_r.at[j - 1, k], {"head": s})

    depth = abuf.shape[3]
    for i in range(nd):
        total = None
        for h in range(m):
            term = jnp.dot(abuf[h].reshape(n * tok, depth), wbuf[h, i], preferred_element_type=F32)
            total = term if total is None else total + term
        part[i] = total.reshape(n, tok, wide).astype(BF16)
        for k in range(1, n):
            to = peer(z, k, n)
            send(part.at[i, to], rbuf.at[k - 1, i], r_s.at[k - 1, i], r_r.at[k - 1, i], {"seq": to})
    for i in range(nd):
        lanes = slice(i * wide, (i + 1) * wide)
        total = part[i, z].astype(F32)
        for k in range(1, n):
            arrived(rbuf.at[k - 1, i], r_s.at[k - 1, i], r_r.at[k - 1, i], {"seq": source(z, k, n)})
            total = total + rbuf[k - 1, i].astype(F32)
        own = (res_ref[:, lanes].astype(F32) + total).astype(BF16)
        own_ref[:, lanes] = own
        st_ref[x, z, i] = own
        mine = st_ref.at[x, z, i]
        for k in range(1, n):
            send(mine, mine, t_s.at[k - 1, i], t_r.at[k - 1, i], {"seq": peer(z, k, n)})
        for j in range(1, m):
            send(mine, mine, tx_s.at[j - 1, 0, i], tx_r.at[j - 1, 0, i], {"head": peer(x, j, m)})
    for i in range(nd):
        for k in range(1, n):
            s = source(z, k, n)
            block = st_ref.at[x, s, i]
            arrived(block, t_s.at[k - 1, i], t_r.at[k - 1, i], {"seq": s})
            for j in range(1, m):
                send(block, block, tx_s.at[j - 1, k, i], tx_r.at[j - 1, k, i], {"head": peer(x, j, m)})
    for k in range(1, n):
        s = source(z, k, n)
        arrived(metas_ref.at[s], me_s.at[k - 1], me_r.at[k - 1], {"seq": s})
    for i in range(nd):
        for j in range(1, m):
            h = source(x, j, m)
            for k in range(n):
                s = source(z, k, n)
                arrived(st_ref.at[h, s, i], tx_s.at[j - 1, k, i], tx_r.at[j - 1, k, i], {"head": h})
    for copy in sends:
        copy.wait_send()


def expert_kernel(n, m, nd, batch, st_ref, metas_ref, gain_ref, wg_ref, wu_ref, out_ref, rows, gates):
    e = pl.program_id(0)
    t = pl.program_id(1)
    experts = rows.shape[0]
    tok, wide = st_ref.shape[3], st_ref.shape[4]
    features = m * nd * wide
    span = batch * tok
    slots = batch * MOST

    @pl.when((e == 0) & (t == 0))
    def _():
        head = lax.axis_index("head")
        r_id = lax.broadcasted_iota(jnp.int32, (span, span), 0)
        c_id = lax.broadcasted_iota(jnp.int32, (span, span), 1)
        before = ((r_id < c_id) & (r_id // tok == c_id // tok)).astype(BF16)
        slot_id = lax.broadcasted_iota(jnp.int32, (slots, span), 0)
        base = (lax.broadcasted_iota(jnp.int32, (1, span), 1) // tok) * MOST
        for b in range(n // batch):
            blocks = slice(b * batch, (b + 1) * batch)
            pieces = [
                st_ref[h, blocks, i].reshape(span, wide).astype(F32) for h in range(m) for i in range(nd)
            ]
            squares = sum(jnp.sum(p * p, axis=1, keepdims=True) for p in pieces)
            factor = lax.rsqrt(squares / features + EPS)
            normed = jnp.concatenate(
                [
                    (p * factor * gain_ref[:, i * wide : (i + 1) * wide].astype(F32)).astype(BF16)
                    for i, p in enumerate(pieces)
                ],
                axis=1,
            )
            meta = jnp.concatenate([metas_ref[b * batch + i] for i in range(batch)], axis=1)
            first, second = meta[0:1], meta[1:2]
            weight = meta[2:3].astype(F32) / 256.0
            for i in range(experts):
                this = head * experts + i
                gate = jnp.where(first == this, weight, 0.0) + jnp.where(second == this, 1.0 - weight, 0.0)
                marked = gate > 0
                spread = jnp.broadcast_to(jnp.where(marked, 1.0, 0.0), (8, span)).astype(BF16)
                rank = jnp.dot(spread, before, preferred_element_type=F32)[0:1].astype(jnp.int32)
                place = jnp.where(marked, rank + base, -1)
                pick = jnp.where(slot_id == place, 1.0, 0.0)
                own = slice(b * slots, (b + 1) * slots)
                rows[i, own] = jnp.dot(pick.astype(BF16), normed, preferred_element_type=F32).astype(BF16)
                gates[i, own] = jnp.sum(pick * gate, axis=1, keepdims=True)

    data = rows[e]
    gate_part = jnp.dot(data, wg_ref[0], preferred_element_type=F32)
    up_part = jnp.dot(data, wu_ref[0], preferred_element_type=F32)
    out_ref[0, 0] = (gates[e] * (gate_part / (1.0 + jnp.exp(-gate_part)) * up_part)).astype(BF16)


def local(
    n, m, nd,
    queries, keys, values, residual_in, out_proj, norm_gain,
    expert_gate, expert_up, routes, gate_numer, sequence_lengths,
):
    tok, feats = queries.shape[1:]
    kv = keys.shape[2]
    share = residual_in.shape[2]
    wide = share // nd
    heads, width, features = out_proj.shape
    depth = heads * width
    experts, _, hidden = expert_gate.shape
    meta = jnp.concatenate([routes[0].T, gate_numer, jnp.zeros((5, tok), jnp.int32)], axis=0)
    vmem = pl.BlockSpec(memory_space=pltpu.VMEM)
    dma = pltpu.SemaphoreType.DMA
    stream_all, own, metas = pl.pallas_call(
        functools.partial(mix_kernel, n, m, nd),
        out_shape=(
            jax.ShapeDtypeStruct((m, n, nd, tok, wide), BF16),
            jax.ShapeDtypeStruct((tok, share), BF16),
            jax.ShapeDtypeStruct((n, 8, tok), jnp.int32),
        ),
        in_specs=[pl.BlockSpec(memory_space=pltpu.SMEM)] + [vmem] * 5 + [pl.BlockSpec(memory_space=pl.ANY)],
        out_specs=(vmem, vmem, vmem),
        scratch_shapes=[
            pltpu.VMEM((n, tok, kv), BF16),
            pltpu.VMEM((n, tok, kv), BF16),
            pltpu.VMEM((m, nd, depth, wide), BF16),
            pltpu.VMEM((n, tok, depth), BF16),
            pltpu.VMEM((m, n, tok, depth), BF16),
            pltpu.VMEM((nd, n, tok, wide), BF16),
            pltpu.VMEM((n - 1, nd, tok, wide), BF16),
            *[dma((n - 1,))] * 6,
            dma((m - 1,)), dma((m - 1,)), dma((m - 1, nd - 1)), dma((m - 1, nd - 1)), dma((nd,)),
            dma((n - 1,)), dma((n - 1,)), dma((m - 1, n)), dma((m - 1, n)),
            dma((n - 1, nd)), dma((n - 1, nd)), dma((n - 1, nd)), dma((n - 1, nd)),
            dma((m - 1, n, nd)), dma((m - 1, n, nd)),
        ],
        compiler_params=pltpu.CompilerParams(
            collective_id=0, has_side_effects=True, vmem_limit_bytes=60 * 1024 * 1024
        ),
    )(
        sequence_lengths, queries[0], keys[0], values[0], meta, residual_in[0],
        out_proj.reshape(depth, features),
    )
    batch = 4 if n % 4 == 0 else n
    tile = min(hidden, 512)
    slots = n * MOST
    weights = pl.BlockSpec((1, features, tile), lambda e, t: (e, 0, t))
    hidden_out = pl.pallas_call(
        functools.partial(expert_kernel, n, m, nd, batch),
        grid=(experts, hidden // tile),
        out_shape=jax.ShapeDtypeStruct((experts, 1, slots, hidden), BF16),
        in_specs=[vmem, vmem, vmem, weights, weights],
        out_specs=pl.BlockSpec((1, 1, slots, tile), lambda e, t: (e, 0, 0, t)),
        scratch_shapes=[pltpu.VMEM((experts, slots, features), BF16), pltpu.VMEM((experts, slots, 1), F32)],
        compiler_params=pltpu.CompilerParams(vmem_limit_bytes=60 * 1024 * 1024),
    )(stream_all, metas, norm_gain[None], expert_gate, expert_up)
    return (own[None], hidden_out)


def solution(mesh):
    seq_spec = P(("grp", "dat"), "seq", "head")
    in_specs = (
        seq_spec, seq_spec, seq_spec, seq_spec,
        P("head", "seq", None), P(),
        P("head", None, "seq"), P("head", None, "seq"),
        P(("grp", "dat"), "seq", None), P(("grp", "dat"), "seq"), P(("grp", "dat")),
    )
    out_specs = (seq_spec, P("head", ("grp", "dat"), None, "seq"))
    body = functools.partial(local, mesh.shape["seq"], mesh.shape["head"], mesh.shape["dat"])
    return jax.shard_map(body, mesh=mesh, in_specs=in_specs, out_specs=out_specs, check_vma=False)
```

time: 294 us -> 92.9 us (0.32)
  waiting for transfers between devices: 179 us -> 0 us
  Pallas kernels: 0 us -> 87 us
  blocking collectives: 51.2 us -> 0 us
  matrix products: 33.7 us -> 0 us
  between operations: 14.7 us -> 1.3 us
  other arithmetic: 7.48 us -> 1.36 us
    all_gather x2 -> x0, waiting for transfers between devices: 165 us -> none  [the longest x1 135 us: local(): proj_part = lax.all_gather(out_proj, 'seq', axis=1, tiled=True)]
    pallas_call x0 -> x2, Pallas kernels: none -> 87 us  [the longest x1 65.6 us: local(): pl.pallas_call(functools.partial(mix_kernel, n, m, nd), out_shape=(jax.Sh...]
    all_gather x4 -> x0, blocking collectives: 46.3 us -> none  [the longest x1 19.9 us: local(): value_part = lax.all_gather(values, 'seq', axis=1, tiled=True)]
    dot_general x7 -> x0, matrix products: 33.7 us -> none  [the longest x2 14 us: expert_rows(): up_part = jnp.dot(rows_in, up_matrix, preferred_element_type=jnp.float32)]
    reduce_scatter x1 -> x0, waiting for transfers between devices: 13.1 us -> none  [local(): lax.psum_scatter(mixed_sum.astype(jnp.bfloat16), 'head', scatter_dimensio...]
    psum x1 -> x0, blocking collectives: 4.93 us -> none  [local(): lax.psum(jnp.sum(as_float * as_float, axis=1, keepdims=True), 'head')]
    gather x4 -> x0, local copies, waits for them, and re-layouts: 2.95 us -> none  [the longest x2 1.56 us: local(): jnp.take(token_gates[:, expert_slot], source[0])]
  transfers between devices with their start and end apart: 3 -> 0, of which waited for: 3 -> 0; matrix products, arithmetic and copies ran while one was open for 2% -> 0% of each run, Pallas kernels for 0% -> 0%
where the time goes in v1:
time: 92.9 us; the launch traced here: 91.7 us
  Pallas kernels  87 us (94%)
  local copies, waits for them, and re-layouts  2.06 us (2%)
  other arithmetic  1.36 us (1%)
  between operations  1.3 us (1%)
    pallas_call x1, Pallas kernels, local(): pl.pallas_call(functools.partial(mix_kernel, n, m, nd), out_shape=(jax.Sh...  65.6 us
    pallas_call x1, Pallas kernels, local(): pl.pallas_call(functools.partial(expert_kernel, n, m, nd, batch), grid=(e...  21.4 us

profile of v1, /device:TPU:20, one launch (start us, length us, event | category | flops | bytes accessed | tf_op | source)
XLA Modules:
  0.0 91.7 jit_solution(9164352374668155257)
XLA Ops:
  1.3 0.1 pad.2.clone
  1.4 1.4 %add_add_fusion.meta_ref = s32[8,64]{1,0:T(8,128)} fusion(s32[1,64]{1,0:T(1,128)} %param.20, s32[2,64]{1,0:T(2,128)} %bitcast.15, s32[8]{0:T(128)S(1)} %pad.2.clone), kind=kLoop, calls=%fused_computation | loop fusion | flops 1024 | bytes 2848 | tf_op jit(solution)/shard_map/concatenate | solution.py:255
  2.7 1.3 %broadcast_in_dim.11.gain_ref = bf16[1,3072]{1,0:T(2,128)(2,1)} reshape(bf16[3072]{0:T(1024)(128)(2,1)} %param.16) | data formatting | bytes 12288 | tf_op jit(solution)/shard_map/broadcast_in_dim | solution.py:300
  4.0 65.6 %shard_map.122 = (bf16[2,4,2,64,768]{4,3,2,1,0:T(8,128)(2,1)}, bf16[64,1536]{1,0:T(8,128)(2,1)}, s32[4,8,64]{2,1,0:T(8,128)}) custom-call(s32[1]{0:T(128)S(6)} %copy.14.len_ref, bf16[64,1536]{1,0:T(8,128)(2,1)} %bitcast.10, bf16[64,256]{1,0:T(8,128)(2,1)} %bitcast.13, bf16[64,256]{1,0:T(8,128)(2,1)} %bitcast.14, s32[8,64]{1,0:T(8,128)} %add_add_fusion.meta_ref, ...), custom_call_target="tpu_custom_call" | custom-call | tf_op jit(solution)/shard_map/pallas_call | solution.py:258
  69.6 0.0 copy-start
  69.6 21.4 %shard_map.123 = bf16[2,1,160,2048]{3,2,1,0:T(8,128)(2,1)} custom-call(bf16[2,4,2,64,768]{4,3,2,1,0:T(8,128)(2,1)} %get-tuple-element.6.st_ref, s32[4,8,64]{2,1,0:T(8,128)} %get-tuple-element.7.metas_ref, bf16[1,3072]{1,0:T(2,128)(2,1)} %broadcast_in_dim.11.gain_ref, bf16[2,3072,2048]{2,1,0:T(8,128)(2,1)} %wg_ref.1, bf16[2,3072,2048]{2,1,0:T(8,128)(2,1)} %wu_ref.1), custom_call_target="tpu_custom_call" | custom-call | tf_op jit(solution)/shard_map/pallas_call | solution.py:292
  91.1 0.0 copy-done
  91.1 0.7 copy.15
  (1 shorter events, 0.0 us)
Async XLA Ops:
  69.6 21.4 %copy-start = (bf16[64,1536]{1,0:T(8,128)(2,1)S(1)}, bf16[64,1536]{1,0:T(8,128)(2,1)}, u32[]{:S(2)}) copy-start(bf16[64,1536]{1,0:T(8,128)(2,1)} %get-tuple-element.5) | copy-start | bytes 589828

commit v2 on v1

--- a/solution.py
+++ b/solution.py
@@ -12,6 +12,7 @@
 MOST = 40
 EPS = 1e-05
 NEG = -1e30
+RING_BYTES = 40 * 1024 * 1024
 MESH = pl.DeviceIdType.MESH
 F32 = jnp.float32
 BF16 = jnp.bfloat16
@@ -19,11 +20,12 @@
 
 def mix_kernel(
     n, m, nd,
-    len_ref, q_ref, k_ref, v_ref, meta_ref, res_ref, w_ref,
-    st_ref, own_ref, metas_ref,
+    len_ref, q_ref, k_ref, v_ref, route_ref, numer_ref, res_ref, gain_ref, w_ref, wg_ref, wu_ref,
+    own_ref, out_ref,
+    st_ref, metas_ref, meta_ref, tiles, acc, rows, picks, gates,
     kbuf, vbuf, wbuf, cut, abuf, part, rbuf,
     k_s, k_r, v_s, v_r, me_s, me_r, w_s, w_r, wf_s, wf_r, wl,
-    a_s, a_r, af_s, af_r, r_s, r_r, t_s, t_r, tx_s, tx_r,
+    a_s, a_r, af_s, af_r, r_s, r_r, t_s, t_r, tx_s, tx_r, tile_s,
 ):
     z = lax.axis_index("seq")
     x = lax.axis_index("head")
@@ -42,6 +44,16 @@
     def source(me, k, size):
         return lax.rem(me - k + size, size)
 
+    experts, hidden = acc.shape[0], acc.shape[3]
+    step = min(hidden, 512)
+    ring = tiles.shape[0]
+    order = [(i, e, u, h) for i in range(nd) for e in range(experts) for u in range(2) for h in range(m)]
+
+    def tile_copy(q):
+        i, e, u, h = order[q]
+        src = (wg_ref, wu_ref)[u].at[e, pl.ds(h * share + i * wide, wide), :]
+        return pltpu.make_async_copy(src, tiles.at[q % ring], tile_s.at[q % ring])
+
     sends = []
 
     def send(src, dst, s_sem, r_sem, where):
@@ -78,6 +90,11 @@
         to = peer(x, j, m)
         start = pl.multiple_of(to * share + c * wide, 128)
         send(w_ref.at[:, pl.ds(start, wide)], wbuf.at[x, c], w_s.at[j - 1], w_r.at[j - 1], {"head": to})
+    for q in range(min(ring, len(order))):
+        tile_copy(q).start()
+    meta_ref[0:2] = route_ref[...].astype(F32)
+    meta_ref[2:3] = numer_ref[...].astype(F32)
+    meta_ref[3:8] = jnp.zeros((5, tok), F32)
     for k in range(1, n):
         send(meta_ref, metas_ref.at[z], me_s.at[k - 1], me_r.at[k - 1], {"seq": peer(z, k, n)})
     kbuf[z] = k_ref[...]
@@ -154,6 +171,29 @@
         for k in range(1, n):
             to = peer(z, k, n)
             send(part.at[i, to], rbuf.at[k - 1, i], r_s.at[k - 1, i], r_r.at[k - 1, i], {"seq": to})
+    for k in range(1, n):
+        s = source(z, k, n)
+        arrived(metas_ref.at[s], me_s.at[k - 1], me_r.at[k - 1], {"seq": s})
+    batch = 4 if n % 4 == 0 else n
+    span = batch * tok
+    part_slots = batch * MOST
+    r_id = lax.broadcasted_iota(jnp.int32, (span, span), 0)
+    c_id = lax.broadcasted_iota(jnp.int32, (span, span), 1)
+    before = ((r_id < c_id) & (r_id // tok == c_id // tok)).astype(BF16)
+    slot_id = lax.broadcasted_iota(jnp.int32, (part_slots, span), 0)
+    base = (lax.broadcasted_iota(jnp.int32, (1, span), 1) // tok) * MOST
+    for b in range(n // batch):
+        meta = jnp.concatenate([metas_ref[b * batch + i] for i in range(batch)], axis=1)
+        weight = meta[2:3] / 256.0
+        for e in range(experts):
+            this = (x * experts + e).astype(F32)
+            gate = jnp.where(meta[0:1] == this, weight, 0.0) + jnp.where(meta[1:2] == this, 1.0 - weight, 0.0)
+            marked = gate > 0
+            spread = jnp.broadcast_to(jnp.where(marked, 1.0, 0.0), (8, span)).astype(BF16)
+            rank = jnp.dot(spread, before, preferred_element_type=F32)[0:1].astype(jnp.int32)
+            pick = jnp.where(slot_id == jnp.where(marked, rank + base, -1), 1.0, 0.0)
+            picks[e, b] = pick.astype(BF16)
+            gates[e, b * part_slots : (b + 1) * part_slots] = jnp.sum(pick * gate, axis=1, keepdims=True)
     for i in range(nd):
         lanes = slice(i * wide, (i + 1) * wide)
         total = part[i, z].astype(F32)
@@ -168,76 +208,76 @@
             send(mine, mine, t_s.at[k - 1, i], t_r.at[k - 1, i], {"seq": peer(z, k, n)})
         for j in range(1, m):
             send(mine, mine, tx_s.at[j - 1, 0, i], tx_r.at[j - 1, 0, i], {"head": peer(x, j, m)})
+    def pass_on(i, k):
+        s = source(z, k, n)
+        block = st_ref.at[x, s, i]
+        arrived(block, t_s.at[k - 1, i], t_r.at[k - 1, i], {"seq": s})
+        for j in range(1, m):
+            send(block, block, tx_s.at[j - 1, k, i], tx_r.at[j - 1, k, i], {"head": peer(x, j, m)})
+
+    squares = [jnp.zeros((span, 1), F32) for _ in range(n // batch)]
+    for k in range(1, n):
+        pass_on(0, k)
     for i in range(nd):
-        for k in range(1, n):
-            s = source(z, k, n)
-            block = st_ref.at[x, s, i]
-            arrived(block, t_s.at[k - 1, i], t_r.at[k - 1, i], {"seq": s})
-            for j in range(1, m):
-                send(block, block, tx_s.at[j - 1, k, i], tx_r.at[j - 1, k, i], {"head": peer(x, j, m)})
-    for k in range(1, n):
-        s = source(z, k, n)
-        arrived(metas_ref.at[s], me_s.at[k - 1], me_r.at[k - 1], {"seq": s})
-    for i in range(nd):
+        ahead = [(i + 1, k) for k in range(1, n)] if i + 1 < nd else []
         for j in range(1, m):
             h = source(x, j, m)
             for k in range(n):
                 s = source(z, k, n)
                 arrived(st_ref.at[h, s, i], tx_s.at[j - 1, k, i], tx_r.at[j - 1, k, i], {"head": h})
+        for h in range(m):
+            start = h * share + i * wide
+            gain = gain_ref[start : start + wide].astype(F32).reshape(1, wide)
+            for b in range(n // batch):
+                block = st_ref[h, b * batch : (b + 1) * batch, i].reshape(span, wide).astype(F32)
+                squares[b] = squares[b] + jnp.sum(block * block, axis=1, keepdims=True)
+                scaled = (block * gain).astype(BF16)
+                for e in range(experts):
+                    rows[e, h, b * part_slots : (b + 1) * part_slots] = jnp.dot(
+                        picks[e, b], scaled, preferred_element_type=F32
+                    ).astype(BF16)
+        for e in range(experts):
+            for u in range(2):
+                q0 = ((i * experts + e) * 2 + u) * m
+                for h in range(m):
+                    tile_copy(q0 + h).wait()
+
+                @pl.loop(0, hidden // step)
+                def _(t):
+                    cols = pl.ds(pl.multiple_of(t * step, step), step)
+                    total = None if i == 0 else acc[e, u, :, cols]
+                    for h in range(m):
+                        term = jnp.dot(rows[e, h], tiles[(q0 + h) % ring, :, cols], preferred_element_type=F32)
+                        total = term if total is None else total + term
+                    acc[e, u, :, cols] = total
+
+                for h in range(m):
+                    if q0 + h + ring < len(order):
+                        tile_copy(q0 + h + ring).start()
+                if ahead:
+                    pass_on(*ahead.pop(0))
+        for item in ahead:
+            pass_on(*item)
+    features = m * share
+    for b in range(n // batch):
+        factor = jnp.broadcast_to(lax.rsqrt(squares[b] / features + EPS), (span, 128))
+        own = slice(b * part_slots, (b + 1) * part_slots)
+        for e in range(experts):
+            slot_factor = jnp.dot(
+                picks[e, b].astype(F32), factor, preferred_element_type=F32, precision=lax.Precision.HIGHEST
+            )[:, 0:1]
+            slot_gate = gates[e, own]
+
+            @pl.loop(0, hidden // step)
+            def _(t):
+                cols = pl.ds(pl.multiple_of(t * step, step), step)
+                gate_part = acc[e, 0, own, cols] * slot_factor
+                up_part = acc[e, 1, own, cols] * slot_factor
+                act = gate_part / (1.0 + jnp.exp(-gate_part))
+                out_ref[e, 0, own, cols] = (slot_gate * (act * up_part)).astype(BF16)
+
     for copy in sends:
         copy.wait_send()
-
-
-def expert_kernel(n, m, nd, batch, st_ref, metas_ref, gain_ref, wg_ref, wu_ref, out_ref, rows, gates):
-    e = pl.program_id(0)
-    t = pl.program_id(1)
-    experts = rows.shape[0]
-    tok, wide = st_ref.shape[3], st_ref.shape[4]
-    features = m * nd * wide
-    span = batch * tok
-    slots = batch * MOST
-
-    @pl.when((e == 0) & (t == 0))
-    def _():
-        head = lax.axis_index("head")
-        r_id = lax.broadcasted_iota(jnp.int32, (span, span), 0)
-        c_id = lax.broadcasted_iota(jnp.int32, (span, span), 1)
-        before = ((r_id < c_id) & (r_id // tok == c_id // tok)).astype(BF16)
-        slot_id = lax.broadcasted_iota(jnp.int32, (slots, span), 0)
-        base = (lax.broadcasted_iota(jnp.int32, (1, span), 1) // tok) * MOST
-        for b in range(n // batch):
-            blocks = slice(b * batch, (b + 1) * batch)
-            pieces = [
-                st_ref[h, blocks, i].reshape(span, wide).astype(F32) for h in range(m) for i in range(nd)
-            ]
-            squares = sum(jnp.sum(p * p, axis=1, keepdims=True) for p in pieces)
-            factor = lax.rsqrt(squares / features + EPS)
-            normed = jnp.concatenate(
-                [
-                    (p * factor * gain_ref[:, i * wide : (i + 1) * wide].astype(F32)).astype(BF16)
-                    for i, p in enumerate(pieces)
-                ],
-                axis=1,
-            )
-            meta = jnp.concatenate([metas_ref[b * batch + i] for i in range(batch)], axis=1)
-            first, second = meta[0:1], meta[1:2]
-            weight = meta[2:3].astype(F32) / 256.0
-            for i in range(experts):
-                this = head * experts + i
-                gate = jnp.where(first == this, weight, 0.0) + jnp.where(second == this, 1.0 - weight, 0.0)
-                marked = gate > 0
-                spread = jnp.broadcast_to(jnp.where(marked, 1.0, 0.0), (8, span)).astype(BF16)
-                rank = jnp.dot(spread, before, preferred_element_type=F32)[0:1].astype(jnp.int32)
-                place = jnp.where(marked, rank + base, -1)
-                pick = jnp.where(slot_id == place, 1.0, 0.0)
-                own = slice(b * slots, (b + 1) * slots)
-                rows[i, own] = jnp.dot(pick.astype(BF16), normed, preferred_element_type=F32).astype(BF16)
-                gates[i, own] = jnp.sum(pick * gate, axis=1, keepdims=True)
-
-    data = rows[e]
-    gate_part = jnp.dot(data, wg_ref[0], preferred_element_type=F32)
-    up_part = jnp.dot(data, wu_ref[0], preferred_element_type=F32)
-    out_ref[0, 0] = (gates[e] * (gate_part / (1.0 + jnp.exp(-gate_part)) * up_part)).astype(BF16)
 
 
 def local(
@@ -252,19 +292,29 @@
     heads, width, features = out_proj.shape
     depth = heads * width
     experts, _, hidden = expert_gate.shape
-    meta = jnp.concatenate([routes[0].T, gate_numer, jnp.zeros((5, tok), jnp.int32)], axis=0)
+    slots = n * MOST
+    batch = 4 if n % 4 == 0 else n
+    ring = min(2 * m * nd * experts, RING_BYTES // (2 * wide * hidden))
     vmem = pl.BlockSpec(memory_space=pltpu.VMEM)
+    hbm = pl.BlockSpec(memory_space=pl.ANY)
     dma = pltpu.SemaphoreType.DMA
-    stream_all, own, metas = pl.pallas_call(
+    own, hidden_out = pl.pallas_call(
         functools.partial(mix_kernel, n, m, nd),
         out_shape=(
-            jax.ShapeDtypeStruct((m, n, nd, tok, wide), BF16),
             jax.ShapeDtypeStruct((tok, share), BF16),
-            jax.ShapeDtypeStruct((n, 8, tok), jnp.int32),
+            jax.ShapeDtypeStruct((experts, 1, slots, hidden), BF16),
         ),
-        in_specs=[pl.BlockSpec(memory_space=pltpu.SMEM)] + [vmem] * 5 + [pl.BlockSpec(memory_space=pl.ANY)],
-        out_specs=(vmem, vmem, vmem),
+        in_specs=[pl.BlockSpec(memory_space=pltpu.SMEM)] + [vmem] * 7 + [hbm] * 3,
+        out_specs=(vmem, vmem),
         scratch_shapes=[
+            pltpu.VMEM((m, n, nd, tok, wide), BF16),
+            pltpu.VMEM((n, 8, tok), F32),
+            pltpu.VMEM((8, tok), F32),
+            pltpu.VMEM((ring, wide, hidden), BF16),
+            pltpu.VMEM((experts, 2, slots, hidden), F32),
+            pltpu.VMEM((experts, m, slots, wide), BF16),
+            pltpu.VMEM((experts, n // batch, batch * MOST, batch * tok), BF16),
+            pltpu.VMEM((experts, slots, 1), F32),
             pltpu.VMEM((n, tok, kv), BF16),
             pltpu.VMEM((n, tok, kv), BF16),
             pltpu.VMEM((m, nd, depth, wide), BF16),
@@ -276,28 +326,15 @@
             dma((m - 1,)), dma((m - 1,)), dma((m - 1, nd - 1)), dma((m - 1, nd - 1)), dma((nd,)),
             dma((n - 1,)), dma((n - 1,)), dma((m - 1, n)), dma((m - 1, n)),
             dma((n - 1, nd)), dma((n - 1, nd)), dma((n - 1, nd)), dma((n - 1, nd)),
-            dma((m - 1, n, nd)), dma((m - 1, n, nd)),
+            dma((m - 1, n, nd)), dma((m - 1, n, nd)), dma((ring,)),
         ],
         compiler_params=pltpu.CompilerParams(
-            collective_id=0, has_side_effects=True, vmem_limit_bytes=60 * 1024 * 1024
+            collective_id=0, has_side_effects=True, vmem_limit_bytes=63 * 1024 * 1024
         ),
     )(
-        sequence_lengths, queries[0], keys[0], values[0], meta, residual_in[0],
-        out_proj.reshape(depth, features),
+        sequence_lengths, queries[0], keys[0], values[0], routes[0].T, gate_numer, residual_in[0],
+        norm_gain, out_proj.reshape(depth, features), expert_gate, expert_up,
     )
-    batch = 4 if n % 4 == 0 else n
-    tile = min(hidden, 512)
-    slots = n * MOST
-    weights = pl.BlockSpec((1, features, tile), lambda e, t: (e, 0, t))
-    hidden_out = pl.pallas_call(
-        functools.partial(expert_kernel, n, m, nd, batch),
-        grid=(experts, hidden // tile),
-        out_shape=jax.ShapeDtypeStruct((experts, 1, slots, hidden), BF16),
-        in_specs=[vmem, vmem, vmem, weights, weights],
-        out_specs=pl.BlockSpec((1, 1, slots, tile), lambda e, t: (e, 0, 0, t)),
-        scratch_shapes=[pltpu.VMEM((experts, slots, features), BF16), pltpu.VMEM((experts, slots, 1), F32)],
-        compiler_params=pltpu.CompilerParams(vmem_limit_bytes=60 * 1024 * 1024),
-    )(stream_all, metas, norm_gain[None], expert_gate, expert_up)
     return (own[None], hidden_out)
 
 

time: 92.9 us -> 88.3 us (0.950); the launches traced: 91.7 us -> 88.1 us
  Pallas kernels: 87 us -> 82.7 us
  local copies, waits for them, and re-layouts: 2.06 us -> 4.14 us
  other arithmetic: 1.36 us -> 0 us
    pallas_call x1 -> x0, Pallas kernels: 21.4 us -> none  [local(): pl.pallas_call(functools.partial(expert_kernel, n, m, nd, batch), grid=(e...]
    pallas_call x1, Pallas kernels: 65.6 us -> 82.7 us  [local(): pl.pallas_call(functools.partial(mix_kernel, n, m, nd), out_shape=(jax.Sh...]
    unnamed x3 -> x2, local copies, waits for them, and re-layouts: 0.68 us -> 4.14 us
    concatenate x1 -> x0, other arithmetic: 1.36 us -> none  [local(): jnp.concatenate([routes[0].T, gate_numer, jnp.zeros((5, tok), jnp.int32)]...]
    broadcast_in_dim x2 -> x0, local copies, waits for them, and re-layouts: 1.3 us -> none  [the longest x1 1.3 us: local(): norm_gain[None]]
where the time goes in v2:
time: 88.3 us; the launch traced here: 88.1 us
  Pallas kernels  82.7 us (94%)
  local copies, waits for them, and re-layouts  4.14 us (5%)
  between operations  1.29 us (1%)
    pallas_call x1, Pallas kernels, local(): pl.pallas_call(functools.partial(mix_kernel, n, m, nd), out_shape=(jax.Sh...  82.7 us
    unnamed x2, local copies, waits for them, and re-layouts  4.14 us

profile of v2, /device:TPU:20, one launch (start us, length us, event | category | flops | bytes accessed | tf_op | source)
XLA Modules:
  0.0 88.1 jit_solution(10950661923619047260)
XLA Ops:
  1.3 82.7 %shard_map.122 = (bf16[64,1536]{1,0:T(8,128)(2,1)}, bf16[2,1,160,2048]{3,2,1,0:T(8,128)(2,1)}) custom-call(s32[1]{0:T(128)S(6)} %copy.15.len_ref, bf16[64,1536]{1,0:T(8,128)(2,1)} %bitcast.10, bf16[64,256]{1,0:T(8,128)(2,1)} %bitcast.13, bf16[64,256]{1,0:T(8,128)(2,1)} %bitcast.14, s32[2,64]{1,0:T(2,128)} %bitcast.15, s32[1,64]{1,0:T(1,128)} %numer_ref.1, ...), custom_call_target="tpu_custom_call" | custom-call | tf_op jit(solution)/shard_map/pallas_call | solution.py:301
  84.0 1.6 %copy.16 = bf16[1,64,1536]{2,1,0:T(8,128)(2,1)} copy(bf16[1,64,1536]{2,1,0:T(8,128)(2,1)} %bitcast.12) | data formatting | bytes 393216
  85.6 2.5 %copy.17 = bf16[2,1,160,2048]{3,2,1,0:T(8,128)(2,1)} copy(bf16[2,1,160,2048]{3,2,1,0:T(8,128)(2,1)} %get-tuple-element.9) | data formatting | bytes 2621440

commit v3 on v2

--- a/solution.py
+++ b/solution.py
@@ -22,7 +22,7 @@
     n, m, nd,
     len_ref, q_ref, k_ref, v_ref, route_ref, numer_ref, res_ref, gain_ref, w_ref, wg_ref, wu_ref,
     own_ref, out_ref,
-    st_ref, metas_ref, meta_ref, tiles, acc, rows, picks, gates,
+    st_ref, metas_ref, meta_ref, tiles, acc, rows, picks, gates, factors,
     kbuf, vbuf, wbuf, cut, abuf, part, rbuf,
     k_s, k_r, v_s, v_r, me_s, me_r, w_s, w_r, wf_s, wf_r, wl,
     a_s, a_r, af_s, af_r, r_s, r_r, t_s, t_r, tx_s, tx_r, tile_s,
@@ -236,48 +236,60 @@
                     rows[e, h, b * part_slots : (b + 1) * part_slots] = jnp.dot(
                         picks[e, b], scaled, preferred_element_type=F32
                     ).astype(BF16)
+        if i == nd - 1:
+            for b in range(n // batch):
+                factor = jnp.broadcast_to(lax.rsqrt(squares[b] / (m * share) + EPS), (span, 128))
+                own = slice(b * part_slots, (b + 1) * part_slots)
+                for e in range(experts):
+                    factors[e, own] = jnp.dot(
+                        picks[e, b].astype(F32), factor, preferred_element_type=F32,
+                        precision=lax.Precision.HIGHEST,
+                    )[:, 0:1]
+
+        def product(e, u, cols):
+            total = None if i == 0 else acc[e, u, :, cols]
+            for h in range(m):
+                q = ((i * experts + e) * 2 + u) * m + h
+                term = jnp.dot(rows[e, h], tiles[q % ring, :, cols], preferred_element_type=F32)
+                total = term if total is None else total + term
+            return total
+
         for e in range(experts):
-            for u in range(2):
-                q0 = ((i * experts + e) * 2 + u) * m
-                for h in range(m):
-                    tile_copy(q0 + h).wait()
-
-                @pl.loop(0, hidden // step)
-                def _(t):
-                    cols = pl.ds(pl.multiple_of(t * step, step), step)
-                    total = None if i == 0 else acc[e, u, :, cols]
-                    for h in range(m):
-                        term = jnp.dot(rows[e, h], tiles[(q0 + h) % ring, :, cols], preferred_element_type=F32)
-                        total = term if total is None else total + term
-                    acc[e, u, :, cols] = total
-
-                for h in range(m):
-                    if q0 + h + ring < len(order):
-                        tile_copy(q0 + h + ring).start()
-                if ahead:
-                    pass_on(*ahead.pop(0))
-        for item in ahead:
-            pass_on(*item)
-    features = m * share
-    for b in range(n // batch):
-        factor = jnp.broadcast_to(lax.rsqrt(squares[b] / features + EPS), (span, 128))
-        own = slice(b * part_slots, (b + 1) * part_slots)
-        for e in range(experts):
-            slot_factor = jnp.dot(
-                picks[e, b].astype(F32), factor, preferred_element_type=F32, precision=lax.Precision.HIGHEST
-            )[:, 0:1]
-            slot_gate = gates[e, own]
+            q0 = (i * experts + e) * 2 * m
+            for q in range(q0, q0 + 2 * m):
+                tile_copy(q).wait()
 
             @pl.loop(0, hidden // step)
             def _(t):
                 cols = pl.ds(pl.multiple_of(t * step, step), step)
-                gate_part = acc[e, 0, own, cols] * slot_factor
-                up_part = acc[e, 1, own, cols] * slot_factor
-                act = gate_part / (1.0 + jnp.exp(-gate_part))
-                out_ref[e, 0, own, cols] = (slot_gate * (act * up_part)).astype(BF16)
-
+                if i < nd - 1:
+                    for u in range(2):
+                        acc[e, u, :, cols] = product(e, u, cols)
+                else:
+                    gate_part = product(e, 0, cols) * factors[e]
+                    up_part = product(e, 1, cols) * factors[e]
+                    act = gate_part / (1.0 + jnp.exp(-gate_part))
+                    out_ref[e, 0, :, cols] = (gates[e] * (act * up_part)).astype(BF16)
+
+            for q in range(q0, q0 + 2 * m):
+                if q + ring < len(order):
+                    tile_copy(q + ring).start()
+            for item in ahead[: -(-(n - 1) // experts)]:
+                pass_on(*item)
+            ahead = ahead[-(-(n - 1) // experts) :]
+        for item in ahead:
+            pass_on(*item)
     for copy in sends:
         copy.wait_send()
+
+
+def place_kernel(own_ref, hidden_ref, own_out, hidden_out, sems):
+    first = pltpu.make_async_copy(own_ref, own_out, sems.at[0])
+    second = pltpu.make_async_copy(hidden_ref, hidden_out, sems.at[1])
+    first.start()
+    second.start()
+    first.wait()
+    second.wait()
 
 
 def local(
@@ -315,6 +327,7 @@
             pltpu.VMEM((experts, m, slots, wide), BF16),
             pltpu.VMEM((experts, n // batch, batch * MOST, batch * tok), BF16),
             pltpu.VMEM((experts, slots, 1), F32),
+            pltpu.VMEM((experts, slots, 1), F32),
             pltpu.VMEM((n, tok, kv), BF16),
             pltpu.VMEM((n, tok, kv), BF16),
             pltpu.VMEM((m, nd, depth, wide), BF16),
@@ -335,6 +348,13 @@
         sequence_lengths, queries[0], keys[0], values[0], routes[0].T, gate_numer, residual_in[0],
         norm_gain, out_proj.reshape(depth, features), expert_gate, expert_up,
     )
+    own, hidden_out = pl.pallas_call(
+        place_kernel,
+        out_shape=tuple(jax.ShapeDtypeStruct(a.shape, a.dtype) for a in (own, hidden_out)),
+        in_specs=[vmem, vmem],
+        out_specs=(hbm, hbm),
+        scratch_shapes=[dma((2,))],
+    )(own, hidden_out)
     return (own[None], hidden_out)
 
 

time: 88.3 us -> 82.9 us (0.939)
  local copies, waits for them, and re-layouts: 4.14 us -> 0 us
  Pallas kernels: 82.7 us -> 81.4 us
    unnamed x2 -> x0, local copies, waits for them, and re-layouts: 4.14 us -> none
    pallas_call x1, Pallas kernels: 82.7 us -> 78.9 us  [local(): pl.pallas_call(functools.partial(mix_kernel, n, m, nd), out_shape=(jax.Sh...]
    pallas_call x0 -> x1, Pallas kernels: none -> 2.57 us  [local(): pl.pallas_call(place_kernel, out_shape=tuple((jax.ShapeDtypeStruct(a.shap...]
where the time goes in v3:
time: 82.9 us; the launch traced here: 82.7 us
  Pallas kernels  81.4 us (98%)
  between operations  1.29 us (2%)
    pallas_call x1, Pallas kernels, local(): pl.pallas_call(functools.partial(mix_kernel, n, m, nd), out_shape=(jax.Sh...  78.9 us
    pallas_call x1, Pallas kernels, local(): pl.pallas_call(place_kernel, out_shape=tuple((jax.ShapeDtypeStruct(a.shap...  2.57 us

profile of v3, /device:TPU:20, one launch (start us, length us, event | category | flops | bytes accessed | tf_op | source)
XLA Modules:
  0.0 82.7 jit_solution(1598975943821503324)
XLA Ops:
  1.3 78.9 %shard_map.122 = (bf16[64,1536]{1,0:T(8,128)(2,1)}, bf16[2,1,160,2048]{3,2,1,0:T(8,128)(2,1)}) custom-call(s32[1]{0:T(128)S(6)} %copy.13.len_ref, bf16[64,1536]{1,0:T(8,128)(2,1)} %bitcast.10, bf16[64,256]{1,0:T(8,128)(2,1)} %bitcast.12, bf16[64,256]{1,0:T(8,128)(2,1)} %bitcast.13, s32[2,64]{1,0:T(2,128)} %bitcast.14, s32[1,64]{1,0:T(1,128)} %numer_ref.1, ...), custom_call_target="tpu_custom_call" | custom-call | tf_op jit(solution)/shard_map/pallas_call | solution.py:313
  80.2 2.6 %shard_map.123 = (bf16[64,1536]{1,0:T(8,128)(2,1)}, bf16[2,1,160,2048]{3,2,1,0:T(8,128)(2,1)}) custom-call(bf16[64,1536]{1,0:T(8,128)(2,1)} %get-tuple-element.6.own_ref, bf16[2,1,160,2048]{3,2,1,0:T(8,128)(2,1)} %get-tuple-element.7.hidden_ref), custom_call_target="tpu_custom_call" | custom-call | tf_op jit(solution)/shard_map/pallas_call | solution.py:351
